TPU v7x, 32 devices: a whole 2x2x4 slice. The times are simulated.
32 devices in a mesh: dp: 8 (over z, y), tensor: 4 (over x, core).
Axes of the slice: x: 2, y: 2, z: 4, core: 2. Of those that a mesh axis runs over, the one named last changes fastest.
Arguments:
- stream_in: float32 [20480, 1024], P(('dp', 'tensor')), may hold values from -27 to 27
- segment_ids: int32 [20480], P('dp'), may hold values from 0 to 103, as said below
- parent_ids: int32 [20480], P('dp'), may hold values from 0 to 95, as said below
- norm_gain_attn: float32 [1024], replicated, may hold values from 0.5 to 1.5
- norm_shift_attn: float32 [1024], replicated, may hold values from -1 to 1
- norm_gain_mlp: float32 [1024], replicated, may hold values from 0.5 to 1.5
- norm_shift_mlp: float32 [1024], replicated, may hold values from -1 to 1
- qkv_weight: float32 [1024, 3072], P('dp', 'tensor'), may hold values from -0.1875 to 0.1875
- qkv_bias: float32 [3072], replicated, may hold values from -1 to 1
- dense_weight: float32 [1024, 1024], P('tensor', 'dp'), may hold values from -3 to 3
- dense_bias: float32 [1024], replicated, may hold values from -1 to 1
- fc_weight: float32 [1024, 4096], P('dp', 'tensor'), may hold values from -0.1875 to 0.1875
- fc_bias: float32 [4096], replicated, may hold values from -1 to 1
- out_weight: float32 [4096, 1024], P('tensor', 'dp'), may hold values from -0.125 to 0.125
- out_bias: float32 [1024], replicated, may hold values from -1 to 1
- out_grad: bfloat16 [20480, 1024], P(('dp', 'tensor')), may hold values from -6 to 6
Outputs:
- output: float32 [20480, 1024], P(('dp', 'tensor'))
- stream_grad: float32 [20480, 1024], P(('dp', 'tensor'))
- gain_attn_grad: float32 [1024], replicated
- shift_attn_grad: float32 [1024], replicated
- gain_mlp_grad: float32 [1024], replicated
- shift_mlp_grad: float32 [1024], replicated
- qkv_weight_grad: float32 [1024, 3072], P('dp', 'tensor')
- qkv_bias_grad: float32 [3072], replicated
- dense_weight_grad: float32 [1024, 1024], P('tensor', 'dp')
- dense_bias_grad: float32 [1024], replicated
- fc_weight_grad: float32 [1024, 4096], P('dp', 'tensor')
- fc_bias_grad: float32 [4096], replicated
- out_weight_grad: float32 [4096, 1024], P('tensor', 'dp')
- out_bias_grad: float32 [1024], replicated
- root_squares: float32 [3], replicated
Inputs may be any that keep to these rules, and one draw needn't show every extreme that they name: `segment_ids`: each tree is 2560 consecutive tokens: its trunk of 1024 tokens first, then 128-token branches and leaves in an order that varies; 4 branches with 2 leaves each; segment numbers are distinct across trees. `parent_ids`: A branch's parent is its tree's trunk, a leaf's parent a branch of the same tree.
All inputs are finite; a program needn't handle non-finite values.
Results may differ from a plain program's by a relative error of at most 0.012.
The roundings to bfloat16 on the way count: a program that leaves them out, or rounds other values in their place, can miss the bound.
Values may be sent and summed in bfloat16 or wider, within the bound.
No kernel may reach another device: no remote copies, remote signals or barrier semaphores. Data moves between devices by JAX's collectives and lax.ppermute only.
A program may use at most 320 MiB of HBM per device.

v0:
```python
import jax
import jax.numpy as jnp
from jax import lax
from jax.sharding import PartitionSpec as P

HD = 64
ROT = 16
TRUNK = 1024
SEG = 128
TREE = 2560
eps_norm = 1e-05
masked_score = -1e30


def contract_first(left, right):
    return lax.dot_general(
        left, right, (((0,), (0,)), ((), ())), preferred_element_type=jnp.float32
    )


def contract_last(left, right):
    return lax.dot_general(
        left, right, (((1,), (1,)), ((), ())), preferred_element_type=jnp.float32
    )


def group_products(left, right, groups):
    rows = left.shape[0]
    inner = left.shape[1] // groups
    parts = jnp.einsum(
        "rgc,gcd->grd",
        left.reshape(rows, groups, inner),
        right.reshape(groups, inner, right.shape[1]),
        preferred_element_type=jnp.float32,
    )
    return jnp.sum(parts.astype(jnp.bfloat16).astype(jnp.float32), axis=0)


def position_tables(segments, parents):
    token_count = segments.shape[0]
    index_all = jnp.arange(token_count, dtype=jnp.int32) % TREE
    root_ids = jnp.repeat(segments.reshape(token_count // TREE, TREE)[:, 0], TREE)
    depth_shift = jnp.where(parents == root_ids, 0, SEG)
    places = jnp.where(
        index_all < TRUNK, index_all, TRUNK + (index_all - TRUNK) % SEG + depth_shift
    )
    half_rot = ROT // 2
    inverse_freq = 10000.0 ** (-(jnp.arange(half_rot, dtype=jnp.float32) * 2.0 / ROT))
    angles = places.astype(jnp.float32)[:, None] * inverse_freq[None, :]
    cosine_table = jnp.concatenate([jnp.cos(angles), jnp.cos(angles)], axis=1)
    sine_table = jnp.concatenate([jnp.sin(angles), jnp.sin(angles)], axis=1)
    return (cosine_table, sine_table, root_ids)


def rotate_forward(field, cosine_table, sine_table):
    half_rot = ROT // 2
    turned_part = field[..., :ROT]
    first_half = turned_part[..., :half_rot]
    second_half = turned_part[..., half_rot:]
    swapped = jnp.concatenate([-second_half, first_half], axis=-1)
    turned = turned_part * cosine_table[:, None, :] + swapped * sine_table[:, None, :]
    return jnp.concatenate([turned, field[..., ROT:]], axis=-1)


def rotate_backward(gradient, cosine_table, sine_table):
    half_rot = ROT // 2
    turned_part = gradient[..., :ROT]
    with_cosine = turned_part * cosine_table[:, None, :]
    with_sine = turned_part * sine_table[:, None, :]
    back = with_cosine + jnp.concatenate(
        [with_sine[..., half_rot:], -with_sine[..., :half_rot]], axis=-1
    )
    return jnp.concatenate([back, gradient[..., ROT:]], axis=-1)


def visible(seg_rows, parent_rows, root_rows, index_rows, seg_cols, index_cols):
    same_seg = (seg_cols[None, :] == seg_rows[:, None]) & (
        index_cols[None, :] <= index_rows[:, None]
    )
    upper_seg = (seg_cols[None, :] == parent_rows[:, None]) & (parent_rows != seg_rows)[:, None]
    rooted_seg = (seg_cols[None, :] == root_rows[:, None]) & (root_rows != seg_rows)[:, None]
    return same_seg | upper_seg | rooted_seg


def block_size():
    return 512


def key_limit(row_end):
    return row_end if row_end <= TRUNK else TREE


def tree_scores(
    queries, key_rows, seg_tree, parent_tree, root_tree, row_start, block_rows, key_end
):
    index_tree = jnp.arange(TREE, dtype=jnp.int32)
    row_end = row_start + block_rows
    allowed = visible(
        seg_tree[row_start:row_end],
        parent_tree[row_start:row_end],
        root_tree[row_start:row_end],
        index_tree[row_start:row_end],
        seg_tree[:key_end],
        index_tree[:key_end],
    )
    raw_scores = jnp.einsum(
        "qhd,khd->hqk",
        queries[row_start:row_end],
        key_rows[:key_end],
        preferred_element_type=jnp.float32,
    )
    return jnp.where(allowed[None], raw_scores * HD ** (-0.5), masked_score)


def forward_tree(pieces):
    queries, key_rows, values, seg_tree, parent_tree, root_tree = pieces
    block_rows = block_size()
    context_parts = []
    total_parts = []
    for block_index in range(TREE // block_rows):
        row_start = block_index * block_rows
        key_end = key_limit(row_start + block_rows)
        scores = tree_scores(
            queries, key_rows, seg_tree, parent_tree, root_tree, row_start, block_rows, key_end
        )
        row_max = jnp.max(scores, axis=-1, keepdims=True)
        exp_total = jnp.sum(jnp.exp(scores - row_max), axis=-1, keepdims=True)
        log_total = row_max + jnp.log(exp_total)
        soft_low = jnp.exp(scores - log_total).astype(jnp.bfloat16)
        context_parts.append(
            jnp.einsum(
                "hqk,khd->qhd", soft_low, values[:key_end], preferred_element_type=jnp.float32
            )
        )
        total_parts.append(log_total[..., 0])
    return (jnp.concatenate(context_parts, axis=0), jnp.concatenate(total_parts, axis=1))


def backward_tree(pieces):
    queries, key_rows, values, seg_tree, parent_tree, root_tree, log_totals, grad_context = pieces
    block_rows = block_size()
    key_grad = jnp.zeros(key_rows.shape, jnp.float32)
    value_grad = jnp.zeros(values.shape, jnp.float32)
    query_parts = []
    for block_index in range(TREE // block_rows):
        row_start = block_index * block_rows
        row_end = row_start + block_rows
        key_end = key_limit(row_end)
        scores = tree_scores(
            queries, key_rows, seg_tree, parent_tree, root_tree, row_start, block_rows, key_end
        )
        soft_full = jnp.exp(scores - log_totals[:, row_start:row_end, None])
        soft_low = soft_full.astype(jnp.bfloat16)
        grad_rows = grad_context[row_start:row_end]
        value_grad = value_grad.at[:key_end].add(
            jnp.einsum("hqk,qhd->khd", soft_low, grad_rows, preferred_element_type=jnp.float32)
        )
        soft_grad = jnp.einsum(
            "qhd,khd->hqk", grad_rows, values[:key_end], preferred_element_type=jnp.float32
        )
        row_delta = jnp.sum(soft_full * soft_grad, axis=-1, keepdims=True)
        score_grad = (soft_full * (soft_grad - row_delta) * HD ** (-0.5)).astype(jnp.bfloat16)
        query_parts.append(
            jnp.einsum(
                "hqk,khd->qhd", score_grad, key_rows[:key_end], preferred_element_type=jnp.float32
            )
        )
        key_grad = key_grad.at[:key_end].add(
            jnp.einsum(
                "hqk,qhd->khd",
                score_grad,
                queries[row_start:row_end],
                preferred_element_type=jnp.float32,
            )
        )
    return (jnp.concatenate(query_parts, axis=0), key_grad, value_grad)


def local(
    stream_in,
    segment_ids,
    parent_ids,
    norm_gain_attn,
    norm_shift_attn,
    norm_gain_mlp,
    norm_shift_mlp,
    qkv_weight,
    qkv_bias,
    dense_weight,
    dense_bias,
    fc_weight,
    fc_bias,
    out_weight,
    out_bias,
    out_grad,
):
    tensor_rank = lax.axis_index("tensor")
    rows_local = stream_in.shape[0]
    group_rows = segment_ids.shape[0]
    qkv_width = qkv_weight.shape[1]
    heads_local = qkv_width // (3 * HD)
    ff_local = fc_weight.shape[1]
    tree_count = group_rows // TREE
    row_mean = jnp.mean(stream_in, axis=-1, keepdims=True)
    centred = stream_in - row_mean
    row_var = jnp.mean(centred * centred, axis=-1, keepdims=True)
    inv_std = lax.rsqrt(row_var + eps_norm)
    normalized = centred * inv_std
    sent_norm = normalized.astype(jnp.bfloat16)
    sent_group = lax.all_gather(sent_norm, "tensor", axis=0, tiled=True)
    qkv_whole, fc_whole, dense_whole, out_whole = (
        lax.all_gather(qkv_weight.astype(jnp.bfloat16), "dp", axis=0, tiled=True),
        lax.all_gather(fc_weight.astype(jnp.bfloat16), "dp", axis=0, tiled=True),
        lax.all_gather(dense_weight.astype(jnp.bfloat16), "dp", axis=1, tiled=True),
        lax.all_gather(out_weight.astype(jnp.bfloat16), "dp", axis=1, tiled=True),
    )
    sent_float = sent_group.astype(jnp.float32)
    normed_attn = (sent_float * norm_gain_attn + norm_shift_attn).astype(jnp.bfloat16)
    normed_mlp = (sent_float * norm_gain_mlp + norm_shift_mlp).astype(jnp.bfloat16)
    qkv_bias_local = lax.dynamic_slice_in_dim(qkv_bias, tensor_rank * qkv_width, qkv_width)
    fc_bias_local = lax.dynamic_slice_in_dim(fc_bias, tensor_rank * ff_local, ff_local)
    qkv = jnp.dot(normed_attn, qkv_whole, preferred_element_type=jnp.float32) + qkv_bias_local
    qkv = qkv.reshape(group_rows, heads_local, 3, HD)
    cosine_table, sine_table, root_ids = position_tables(segment_ids, parent_ids)
    queries = rotate_forward(qkv[:, :, 0], cosine_table, sine_table).astype(jnp.bfloat16)
    key_rows = rotate_forward(qkv[:, :, 1], cosine_table, sine_table).astype(jnp.bfloat16)
    values = qkv[:, :, 2].astype(jnp.bfloat16)
    tree_shape = (tree_count, TREE, heads_local, HD)
    tree_pieces = (
        queries.reshape(tree_shape),
        key_rows.reshape(tree_shape),
        values.reshape(tree_shape),
        segment_ids.reshape(tree_count, TREE),
        parent_ids.reshape(tree_count, TREE),
        root_ids.reshape(tree_count, TREE),
    )
    context, log_totals = lax.map(forward_tree, tree_pieces)
    context_low = context.reshape(group_rows, heads_local * HD).astype(jnp.bfloat16)
    hidden = jnp.dot(normed_mlp, fc_whole, preferred_element_type=jnp.float32) + fc_bias_local
    activated = jax.nn.gelu(hidden, approximate=False).astype(jnp.bfloat16)
    context_own, activated_own = (
        lax.all_to_all(context_low, "tensor", split_axis=0, concat_axis=1, tiled=True),
        lax.all_to_all(activated, "tensor", split_axis=0, concat_axis=1, tiled=True),
    )
    dense_every, out_every = (
        lax.all_gather(dense_whole, "tensor", axis=0, tiled=True),
        lax.all_gather(out_whole, "tensor", axis=0, tiled=True),
    )
    group_count = lax.axis_size("tensor")
    attn_sum = group_products(context_own, dense_every, group_count)
    mlp_sum = group_products(activated_own, out_every, group_count)
    attn_out = attn_sum + dense_bias
    mlp_out = mlp_sum + out_bias
    output = stream_in + attn_out + mlp_out
    grad_group = lax.all_gather(out_grad, "tensor", axis=0, tiled=True)
    grad_activated = contract_last(grad_group, out_whole)
    out_weight_part = contract_first(activated, grad_group)
    hidden_primal, gelu_pullback = jax.vjp(
        lambda field: jax.nn.gelu(field, approximate=False), hidden
    )
    grad_hidden = gelu_pullback(grad_activated)[0].astype(jnp.bfloat16)
    fc_bias_part = jnp.sum(grad_hidden.astype(jnp.float32), axis=0)
    fc_weight_part = contract_first(normed_mlp, grad_hidden)
    grad_normed_mlp = contract_last(grad_hidden, fc_whole)
    grad_context = contract_last(grad_group, dense_whole).astype(jnp.bfloat16)
    dense_weight_part = contract_first(context_low, grad_group)
    query_grad, key_grad, value_grad = lax.map(
        backward_tree, tree_pieces + (log_totals, grad_context.reshape(tree_shape))
    )
    query_grad = rotate_backward(
        query_grad.reshape(group_rows, heads_local, HD), cosine_table, sine_table
    )
    key_grad = rotate_backward(
        key_grad.reshape(group_rows, heads_local, HD), cosine_table, sine_table
    )
    value_grad = value_grad.reshape(group_rows, heads_local, HD)
    grad_qkv = jnp.stack([query_grad, key_grad, value_grad], axis=2).reshape(group_rows, qkv_width)
    grad_qkv = grad_qkv.astype(jnp.bfloat16)
    qkv_bias_part = jnp.sum(grad_qkv.astype(jnp.float32), axis=0)
    qkv_weight_part = contract_first(normed_attn, grad_qkv)
    grad_normed_attn = contract_last(grad_qkv, qkv_whole)
    gain_attn_part = jnp.sum(grad_normed_attn * sent_float, axis=0)
    shift_attn_part = jnp.sum(grad_normed_attn, axis=0)
    gain_mlp_part = jnp.sum(grad_normed_mlp * sent_float, axis=0)
    shift_mlp_part = jnp.sum(grad_normed_mlp, axis=0)
    grad_sent_part = grad_normed_attn * norm_gain_attn + grad_normed_mlp * norm_gain_mlp
    grad_sent = lax.psum_scatter(
        grad_sent_part.astype(jnp.bfloat16), "tensor", scatter_dimension=0, tiled=True
    ).astype(jnp.float32)
    mean_grad = jnp.mean(grad_sent, axis=-1, keepdims=True)
    mean_cross = jnp.mean(grad_sent * normalized, axis=-1, keepdims=True)
    stream_grad = out_grad.astype(jnp.float32) + inv_std * (
        grad_sent - mean_grad - normalized * mean_cross
    )
    qkv_weight_grad, fc_weight_grad, dense_weight_grad, out_weight_grad = (
        lax.psum_scatter(
            qkv_weight_part.astype(jnp.bfloat16), "dp", scatter_dimension=0, tiled=True
        ).astype(jnp.float32),
        lax.psum_scatter(
            fc_weight_part.astype(jnp.bfloat16), "dp", scatter_dimension=0, tiled=True
        ).astype(jnp.float32),
        lax.psum_scatter(
            dense_weight_part.astype(jnp.bfloat16), "dp", scatter_dimension=1, tiled=True
        ).astype(jnp.float32),
        lax.psum_scatter(
            out_weight_part.astype(jnp.bfloat16), "dp", scatter_dimension=1, tiled=True
        ).astype(jnp.float32),
    )
    residual_part = jnp.sum(out_grad.astype(jnp.float32), axis=0)
    qkv_bias_spread = lax.dynamic_update_slice(
        jnp.zeros(qkv_bias.shape, jnp.float32), qkv_bias_part, (tensor_rank * qkv_width,)
    )
    fc_bias_spread = lax.dynamic_update_slice(
        jnp.zeros(fc_bias.shape, jnp.float32), fc_bias_part, (tensor_rank * ff_local,)
    )
    (
        gain_attn_grad,
        shift_attn_grad,
        gain_mlp_grad,
        shift_mlp_grad,
        residual_grad,
        qkv_bias_grad,
        fc_bias_grad,
        output_square,
        attn_square,
        mlp_square,
    ) = lax.psum(
        (
            gain_attn_part,
            shift_attn_part,
            gain_mlp_part,
            shift_mlp_part,
            residual_part,
            qkv_bias_spread,
            fc_bias_spread,
            jnp.sum(output * output),
            jnp.sum(attn_out * attn_out),
            jnp.sum(mlp_out * mlp_out),
        ),
        ("dp", "tensor"),
    )
    count_all = float(
        rows_local * lax.axis_size("dp") * lax.axis_size("tensor") * stream_in.shape[1]
    )
    root_squares = jnp.sqrt(jnp.stack([output_square, attn_square, mlp_square]) / count_all)
    return (
        output,
        stream_grad,
        gain_attn_grad,
        shift_attn_grad,
        gain_mlp_grad,
        shift_mlp_grad,
        qkv_weight_grad,
        qkv_bias_grad,
        dense_weight_grad,
        residual_grad,
        fc_weight_grad,
        fc_bias_grad,
        out_weight_grad,
        residual_grad,
        root_squares,
    )


def solution(mesh):
    placed = (
        P(("dp", "tensor"), None),
        P("dp"),
        P("dp"),
        P(),
        P(),
        P(),
        P(),
        P("dp", "tensor"),
        P(),
        P("tensor", "dp"),
        P(),
        P("dp", "tensor"),
        P(),
        P("tensor", "dp"),
        P(),
        P(("dp", "tensor"), None),
    )
    return jax.shard_map(
        local,
        mesh=mesh,
        in_specs=placed,
        out_specs=(
            P(("dp", "tensor"), None),
            P(("dp", "tensor"), None),
            P(),
            P(),
            P(),
            P(),
            P("dp", "tensor"),
            P(),
            P("tensor", "dp"),
            P(),
            P("dp", "tensor"),
            P(),
            P("tensor", "dp"),
            P(),
            P(),
        ),
        check_vma=False,
    )
```

profile of v0, /device:TPU:0, one launch (start us, length us, event | category | flops | bytes accessed | tf_op | source)
XLA Modules:
  0.0 1078.6 jit_solution(15230396105723233312)
XLA Ops:
  18.3 33.0 %all_gather.26 = bf16[256,1024]{1,0:T(8,128)(2,1)} all-gather(bf16[256,128]{1,0:T(8,128)(2,1)S(1)} %convert_element_type.175), channel_id=1, replica_groups=mesh['dp'=8,'tensor'=4] {'dp'}, dimensions={1}, use_global_device_ids=true | all-gather | bytes 589824 | tf_op jit(solution)/shard_map/all_gather | solution.py:214
  59.7 9.0 fusion.112
  68.8 34.1 %all-gather.8.cloned.1.call-done = bf16[2560,1024]{1,0:T(8,128)(2,1)} async-done(((bf16[640,1024]{1,0:T(8,128)(2,1)}), bf16[2560,1024]{1,0:T(8,128)(2,1)}) %all-gather.8.cloned.1.call-update) | async-done | bytes 5242896 | tf_op jit(solution)/shard_map/all_gather | solution.py:210
  102.9 6.9 convolution_add_fusion
  109.8 2.5 copy.67
  116.5 28.5 %all-gather.20.cloned.1.call-done = bf16[2560,1024]{1,0:T(8,128)(2,1)} async-done(((bf16[640,1024]{1,0:T(8,128)(2,1)}), bf16[2560,1024]{1,0:T(8,128)(2,1)}) %all-gather.20.cloned.1.call-update) | async-done | bytes 5242896 | tf_op jit(solution)/shard_map/all_gather | solution.py:255
  145.0 4.3 convolution_convert_fusion
  155.1 3.9 fusion.253
  161.0 8.7 fusion.207
  169.7 9.8 fusion.204
  179.4 4.3 fusion.213
  185.6 5.5 fusion.248
  192.8 3.2 copy-done.2
  196.0 2.4 exponential_reduce_fusion.3
  198.5 18.0 %fusion.218 = f32[2560,4,64]{0,2,1:T(8,128)} fusion(f32[2560,4,64]{0,2,1:T(8,128)} %fusion.204, f32[4,512,1024]{2,1,0:T(8,128)} %fusion.248, f32[4,512,1024]{2,1,0:T(8,128)} %copy-done.2, f32[4,512]{1,0:T(4,128)S(1)} %log_add_fusion.3, pred[512,1024]{1,0:T(8,128)(4,1)S(1)} %and_or_fusion, bf16[2560,4,48]{0,2,1:T(8,128)(2,1)S(1)} %slice.741, ...), kind=kOutput, calls=%fused_computation.211 | convolution fusion | flops 292555776 | bytes 36454400 | tf_op jit(solution)/shard_map/while/body/eval_jaxpr/hqk,khd->qhd/dot_general | solution.py:164
  216.6 23.2 %fusion.197 = f32[2560,4,64]{0,2,1:T(8,128)} fusion(f32[2560,4,64]{0,2,1:T(8,128)} %scatter-add.14, f32[4,512,1024]{2,1,0:T(8,128)} %fusion.248, f32[4,512,1024]{2,1,0:T(8,128)} %copy-done.2, f32[4,512]{1,0:T(4,128)S(1)} %log_add_fusion.3, pred[512,1024]{1,0:T(8,128)(4,1)S(1)} %and_or_fusion, bf16[2560,4,48]{0,2,1:T(8,128)(2,1)S(1)} %slice.742, ...), kind=kOutput, calls=%fused_computation.187 | convolution fusion | flops 292293632 | bytes 38027264 | tf_op jit(solution)/shard_map/while/body/eval_jaxpr/hqk,qhd->khd/dot_general | solution.py:169
  239.8 10.1 fusion.247
  249.9 9.0 fusion.246
  258.8 8.6 fusion.245
  267.5 5.6 fusion.10
  273.1 7.3 exponential_reduce_fusion
  280.5 5.5 fusion.8
  286.0 7.1 exponential_reduce_fusion.2
  293.5 5.5 fusion.9
  299.0 7.1 exponential_reduce_fusion.1
  306.5 40.6 %fusion.140 = f32[2560,4,64]{0,2,1:T(8,128)} fusion(f32[4,512,2560]{2,1,0:T(8,128)} %fusion.246, f32[4,512,2560]{2,1,0:T(8,128)} %copy-done.4, f32[4,512]{1,0:T(4,128)S(1)} %log_add_fusion.1, pred[512,2560]{1,0:T(8,128)(4,1)} %get-tuple-element.354, bf16[2560,4,48]{0,2,1:T(8,128)(2,1)S(1)} %slice.742, bf16[2560,4,16]{0,2,1:T(8,128)(2,1)S(1)} %get-tuple-element.341), kind=kOutput, calls=%fused_computation.132 | convolution fusion | flops 729289216 | bytes 90456064 | tf_op jit(solution)/shard_map/while/body/eval_jaxpr/hqk,qhd->khd/dot_general | solution.py:169
  347.1 38.3 %fusion.236 = f32[2560,4,64]{0,2,1:T(8,128)} fusion(f32[2560,4,64]{0,2,1:T(8,128)} %fusion.218, f32[4,512,2560]{2,1,0:T(8,128)} %fusion.247, f32[4,512,2560]{2,1,0:T(8,128)} %copy-done.5, f32[4,512]{1,0:T(4,128)S(1)} %log_add_fusion.2, pred[512,2560]{1,0:T(8,128)(4,1)} %get-tuple-element.353, bf16[2560,4,48]{0,2,1:T(8,128)(2,1)S(1)} %slice.741, ...), kind=kOutput, calls=%fused_computation.217 | convolution fusion | flops 731386368 | bytes 88358912 | tf_op jit(solution)/shard_map/while/body/eval_jaxpr/hqk,khd->qhd/dot_general | solution.py:164
  385.4 37.8 %fusion.230 = f32[2560,4,64]{0,2,1:T(8,128)} fusion(f32[2560,4,64]{0,2,1:T(8,128)} %fusion.236, f32[4,512,2560]{2,1,0:T(8,128)} %fusion.246, f32[4,512,2560]{2,1,0:T(8,128)} %copy-done.4, f32[4,512]{1,0:T(4,128)S(1)} %log_add_fusion.1, pred[512,2560]{1,0:T(8,128)(4,1)} %get-tuple-element.354, bf16[2560,4,48]{0,2,1:T(8,128)(2,1)S(1)} %slice.741, ...), kind=kOutput, calls=%fused_computation.215 | convolution fusion | flops 731386368 | bytes 88358912 | tf_op jit(solution)/shard_map/while/body/eval_jaxpr/hqk,khd->qhd/dot_general | solution.py:164
  423.2 40.6 %fusion.137 = f32[2560,4,64]{0,2,1:T(8,128)} fusion(bf16[512,4,64]{0,2,1:T(8,128)(2,1)S(1)} %copy-done.43, f32[4,512,2560]{2,1,0:T(8,128)} %fusion.245, f32[4,512,2560]{2,1,0:T(8,128)} %copy-done.3, f32[4,512]{1,0:T(4,128)S(1)} %log_add_fusion, pred[512,2560]{1,0:T(8,128)(4,1)} %get-tuple-element.352), kind=kOutput, calls=%fused_computation.131 | convolution fusion | flops 728764928 | bytes 46145536 | tf_op jit(solution)/shard_map/while/body/eval_jaxpr/hqk,qhd->khd/dot_general | solution.py:169
  463.8 37.8 %fusion.224 = f32[2560,4,64]{0,2,1:T(8,128)} fusion(f32[2560,4,64]{0,2,1:T(8,128)} %fusion.230, f32[4,512,2560]{2,1,0:T(8,128)} %fusion.245, f32[4,512,2560]{2,1,0:T(8,128)} %copy-done.3, f32[4,512]{1,0:T(4,128)S(1)} %log_add_fusion, pred[512,2560]{1,0:T(8,128)(4,1)} %get-tuple-element.352, bf16[2560,4,48]{0,2,1:T(8,128)(2,1)S(1)} %slice.741, ...), kind=kOutput, calls=%fused_computation.213 | convolution fusion | flops 731386368 | bytes 88358912 | tf_op jit(solution)/shard_map/while/body/eval_jaxpr/hqk,khd->qhd/dot_general | solution.py:164
  501.7 41.5 %fusion.156 = f32[2560,4,64]{0,2,1:T(8,128)} fusion(f32[2560,4,64]{0,2,1:T(8,128)} %fusion.137, f32[2560,4,64]{0,2,1:T(8,128)} %fusion.140, f32[2560,4,64]{0,2,1:T(8,128)} %fusion.197, f32[4,512,2560]{2,1,0:T(8,128)} %fusion.247, f32[4,512,2560]{2,1,0:T(8,128)} %copy-done.5, f32[4,512]{1,0:T(4,128)S(1)} %log_add_fusion.2, ...), kind=kOutput, calls=%fused_computation.143 | convolution fusion | flops 731255296 | bytes 98320384 | tf_op jit(solution)/shard_map/while/body/eval_jaxpr/hqk,qhd->khd/dot_general | solution.py:169
  543.2 2.7 slice.646
  545.9 2.6 slice.642
  548.5 2.4 slice_multiply_fusion.3
  551.3 5.0 fusion.193
  557.3 2.3 fusion.214
  559.7 11.7 %fusion.149 = f32[2560,4,64]{0,2,1:T(8,128)} fusion(f32[2560,4,64]{0,2,1:T(8,128)S(1)} %fusion.193, bf16[512,4,64]{0,2,1:T(8,128)(2,1)S(1)} %bitcast.184, f32[4,512,2560]{2,1,0:T(8,128)} %copy-done.5, f32[4,512]{1,0:T(4,128)S(1)} %log_add_fusion.2, pred[512,2560]{1,0:T(8,128)(4,1)S(1)} %copy-done.13), kind=kOutput, calls=%fused_computation.140 | convolution fusion | flops 692715520 | bytes 27795456 | tf_op jit(solution)/shard_map/while/body/eval_jaxpr/hqk,qhd->khd/dot_general | solution.py:156
  571.4 9.8 fusion.212
  581.3 10.4 fusion.211
  591.7 9.8 fusion.210
  602.7 2.3 convolution_convert_fusion.2
  610.6 10.2 fusion.148
  620.8 10.4 fusion.147
  635.1 9.2 fusion.186
  644.4 11.2 %fusion.161 = f32[2560,1024]{1,0:T(8,128)} fusion(bf16[1024,1024]{1,0:T(8,128)(2,1)} %all-gather.14.cloned.1.call-done, bf16[2560,1024]{1,0:T(8,128)(2,1)} %all-gather.8.cloned.1.call-done, f32[1024]{0:T(1024)S(1)} %copy-done.60, f32[1024]{0:T(1024)S(1)} %copy-done.63), kind=kOutput, calls=%fused_computation.145 | convolution fusion | flops 5379194880 | bytes 17833984 | tf_op jit(solution)/shard_map/dot_general | solution.py:239
  655.6 33.9 %convert_reduce_fusion = (f32[1024]{0:T(1024)S(1)}, bf16[2560,1024]{1,0:T(8,128)(2,1)}, f32[2560,1024]{1,0:T(8,128)}) fusion(f32[2560,1024]{1,0:T(8,128)} %fusion.161, f32[1024]{0:T(1024)S(1)} %copy-done.51, bf16[2560,1024]{1,0:T(8,128)(2,1)} %all-gather.20.cloned.1.call-done, bf16[1024,1024]{1,0:T(8,128)(2,1)} %all-gather.16.cloned.1.call-done), kind=kOutput, calls=%fused_computation.47 | convolution fusion | flops 5565316096 | bytes 33562624 | tf_op jit(solution)/shard_map/dot_general | solution.py:22
  689.6 12.3 %multiply_convert_fusion.3 = bf16[2560,1024]{1,0:T(8,128)(2,1)} fusion(f32[2560,1024]{1,0:T(8,128)} %get-tuple-element.316, f32[2560,1024]{1,0:T(8,128)} %fusion.161, f32[1024]{0:T(1024)S(1)} %copy-done.51), kind=kLoop, calls=%fused_computation.51 | loop fusion | flops 10485760 | bytes 26218496 | tf_op jit(solution)/shard_map/convert_element_type | solution.py:240
  701.8 9.4 convolution_convert_fusion.1
  711.2 2.6 copy.64
  713.9 10.2 fusion.183
  724.8 7.2 fusion.336
  732.1 15.2 %fusion.328 = (f32[1024]{0:T(1024)S(1)}, f32[1024]{0:T(1024)S(1)}, bf16[2560,1024]{1,0:T(8,128)(2,1)}, f32[1024]{0:T(1024)S(1)}, f32[1024]{0:T(1024)S(1)}) fusion(bf16[2560,1024]{1,0:T(8,128)(2,1)} %all-gather.8.cloned.1.call-done, f32[1024]{0:T(1024)S(1)} %copy-done.63, f32[2560,1024]{1,0:T(8,128)S(1)} %fusion.336, f32[1024]{0:T(1024)S(1)} %copy-done.62, ...), kind=kOutput, calls=%fused_computation.332 | convolution fusion | flops 5397540864 | bytes 28336128 | tf_op jit(solution)/shard_map/dot_general | solution.py:22
  750.4 19.7 %all_to_all.29 = bf16[4,640,256]{2,1,0:T(8,128)(2,1)S(1)} all-to-all(bf16[4,640,256]{2,1,0:T(8,128)(2,1)S(1)} %copy.52), channel_id=1, replica_groups=mesh['dp'=8,'tensor'=4] {'tensor'}, dimensions={0} | all-to-all | bytes 2621440 | tf_op jit(solution)/shard_map/all_to_all | solution.py:242
  770.1 5.3 all-to-all-start.1
  776.1 4.8 convert_reduce_fusion.2
  784.2 50.7 %reduce-scatter.18.cloned.1.call-done = bf16[128,1024]{1,0:T(8,128)(2,1)} async-done(((bf16[1024,1024]{1,0:T(8,128)(2,1)}), bf16[128,1024]{1,0:T(8,128)(2,1)}) %reduce-scatter.18.cloned.1.call-update) | async-done | bytes 262160
  836.9 69.0 %reduce-scatter.14.cloned.1.call-done = bf16[128,1024]{1,0:T(8,128)(2,1)} async-done(((bf16[1024,1024]{1,0:T(8,128)(2,1)}), bf16[128,1024]{1,0:T(8,128)(2,1)}) %reduce-scatter.14.cloned.1.call-update) | async-done | bytes 262160 | tf_op jit(solution)/shard_map/reduce_scatter | solution.py:299
  907.6 57.1 %all-gather.18.cloned.1.call-done = bf16[4096,1024]{1,0:T(8,128)(2,1)} async-done(((bf16[1024,1024]{1,0:T(8,128)(2,1)}), bf16[4096,1024]{1,0:T(8,128)(2,1)}) %all-gather.18.cloned.1.call-update) | async-done | bytes 8388624 | tf_op jit(solution)/shard_map/all_gather | solution.py:247
  964.7 11.9 %convert_reduce_fusion.1 = f32[640,1024]{1,0:T(8,128)} fusion(bf16[4,1024,1024]{2,1,0:T(8,128)(2,1)} %bitcast.191, bf16[4,640,1024]{2,1,0:T(8,128)(2,1)} %all-to-all-done.1), kind=kOutput, calls=%fused_computation.50 | convolution fusion | flops 5375918080 | bytes 16252928 | tf_op jit(solution)/shard_map/rgc,gcd->grd/dot_general | solution.py:30
  976.6 41.9 %reduce-scatter.10.cloned.1.call-done = bf16[640,1024]{1,0:T(8,128)(2,1)} async-done(((bf16[2560,1024]{1,0:T(8,128)(2,1)}), bf16[640,1024]{1,0:T(8,128)(2,1)}) %reduce-scatter.10.cloned.1.call-update) | async-done | bytes 1310736 | tf_op jit(solution)/shard_map/reduce_scatter | solution.py:287
  1018.5 2.4 convert_reduce_fusion.4
  1021.0 6.7 multiply_reduce_fusion.7
  1027.6 40.9 %all-reduce.2 = (f32[1024]{0:T(1024)}, f32[1024]{0:T(1024)}, f32[1024]{0:T(1024)}, f32[1024]{0:T(1024)}, f32[3072]{0:T(1024)}, /*index=5*/f32[1024]{0:T(1024)S(1...) all-reduce(f32[1024]{0:T(1024)S(1)} %get-tuple-element.320, ...), channel_id=1, replica_groups=mesh['dp'=8,'tensor'=4] {'dp','tensor'}, use_global_device_ids=true, to_apply=%region_23.24 | all-reduce | flops 12291 | bytes 98328 | tf_op jit(solution)/shard_map/psum | solution.py:327
  1068.5 2.4 fusion.272
  (244 shorter events, 59.7 us)
Async XLA Ops:
  7.2 6.2 copy-start
  7.2 61.6 %all-gather.10.cloned.1.call-start = ((), (), s32[]{:S(2)}) async-start(), calls=%async_computation.8 | async-start | bytes 1769472 | tf_op jit(solution)/shard_map/all_gather | solution.py:212
  9.1 93.8 %all-gather.8.cloned.1.call-start = ((), (), s32[]{:S(2)}) async-start(), calls=%async_computation.7 | async-start | bytes 6553600 | tf_op jit(solution)/shard_map/all_gather | solution.py:210
  11.1 7.1 copy-start.45
  11.1 7.1 copy-start.44
  13.3 38.1 %copy-start.42 = (s32[2560]{0:T(1024)S(1)}, s32[2560]{0:T(1024)}, u32[]{:S(2)}) copy-start(s32[2560]{0:T(1024)} %param.49) | copy-start | bytes 30724
  13.3 40.0 %copy-start.47 = (s32[2560]{0:T(1024)S(1)}, s32[2560]{0:T(1024)}, u32[]{:S(2)}) copy-start(s32[2560]{0:T(1024)} %param.50) | copy-start | bytes 30724
  13.4 44.5 %copy-start.48 = (f32[640]{0:T(1024)}, f32[640]{0:T(1024)S(1)}, u32[]{:S(2)}) copy-start(f32[640]{0:T(1024)S(1)} %add_rsqrt_fusion) | copy-start | bytes 7684
  13.4 44.9 %slice-start.2 = ((s32[2560]{0:T(1024)}), s32[1024]{0:T(1024)S(1)}, s32[]{:S(2)}) async-start(s32[2560]{0:T(1024)} %param.49), calls=%async_computation.21 | async-start | bytes 8192 | tf_op jit(solution)/shard_map/while/body/eval_jaxpr/slice | solution.py:103
  14.8 88.1 %copy-start.58 = (f32[1024]{0:T(1024)S(1)}, f32[1024]{0:T(1024)}, u32[]{:S(2)}) copy-start(f32[1024]{0:T(1024)} %param.52) | copy-start | bytes 12292
  14.8 88.1 %copy-start.61 = (f32[1024]{0:T(1024)S(1)}, f32[1024]{0:T(1024)}, u32[]{:S(2)}) copy-start(f32[1024]{0:T(1024)} %param.51) | copy-start | bytes 12292
  14.8 130.1 %all-gather.20.cloned.1.call-start = ((), (), s32[]{:S(2)}) async-start(), calls=%async_computation.13 | async-start | bytes 6553600 | tf_op jit(solution)/shard_map/all_gather | solution.py:255
  15.6 628.8 %all-gather.14.cloned.1.call-start = ((), (), s32[]{:S(2)}) async-start(), calls=%async_computation.10 | async-start | bytes 2359296 | tf_op jit(solution)/shard_map/all_gather | solution.py:213
  16.4 639.3 %all-gather.16.cloned.1.call-start = ((), (), s32[]{:S(2)}) async-start(), calls=%async_computation.11 | async-start | bytes 2359296 | tf_op jit(solution)/shard_map/all_gather | solution.py:215
  18.2 757.9 %all-gather.12.cloned.1.call-start = ((), (), s32[]{:S(2)}) async-start(), calls=%async_computation.9 | async-start | bytes 2621440 | tf_op jit(solution)/shard_map/all_gather | solution.py:246
  51.3 729.6 %reduce-scatter.16.cloned.1.call-start = ((), (), s32[]{:S(2)}) async-start(), calls=%async_computation.17 | async-start | bytes 589824
  59.7 156.8 %copy-start.14 = (pred[512,1024]{1,0:T(8,128)(4,1)}, pred[512,1024]{1,0:T(8,128)(4,1)S(1)}, u32[]{:S(2)}) copy-start(pred[512,1024]{1,0:T(8,128)(4,1)S(1)} %and_or_fusion) | copy-start | bytes 1572868
  144.9 5.3 copy-start.19
  144.9 5.3 copy-start.21
  144.9 5.3 copy-start.23
  144.9 5.3 copy-start.24
  144.9 5.3 copy-start.25
  145.0 5.3 copy-start.26
  179.4 6.2 copy-start.36
  198.5 18.1 %copy-start.52 = (f32[4,512]{1,0:T(4,128)}, f32[4,512]{1,0:T(4,128)S(1)}, u32[]{:S(2)}) copy-start(f32[4,512]{1,0:T(4,128)S(1)} %log_add_fusion.3) | copy-start | bytes 24580
  216.5 23.2 %copy-start.34 = (bf16[512,256]{0,1:T(8,128)(2,1)S(1)}, bf16[512,256]{0,1:T(8,128)(2,1)}, u32[]{:S(2)}) copy-start(bf16[512,256]{0,1:T(8,128)(2,1)} %get-tuple-element.334) | copy-start | bytes 786436
  239.8 10.1 copy-start.6
  239.8 10.1 copy-start.32
  249.9 9.0 copy-start.30
  258.8 8.7 copy-start.43
  273.1 7.4 copy-start.3
  286.0 7.4 copy-start.5
  299.0 7.4 copy-start.4
  501.7 46.8 %copy-start.22 = (f32[2560,16]{0,1:T(8,128)S(1)}, f32[2560,16]{0,1:T(8,128)}, u32[]{:S(2)}) copy-start(f32[2560,16]{0,1:T(8,128)} %get-tuple-element.391) | copy-start | bytes 491524
  543.1 7.8 copy-start.40
  543.1 8.1 copy-start.15
  543.2 8.1 copy-start.37
  543.2 8.1 copy-start.53
  548.5 7.8 slice-start
  551.2 5.1 slice-start.1
  551.2 5.8 copy-start.7
  551.2 6.1 copy-start.27
  571.4 9.8 copy-start.12
  581.3 10.4 copy-start.11
  581.3 21.4 %slice-start.3 = ((s8[5242880]{0:T(1024)(128)(4,1)}), s8[4194304]{0:T(1024)(128)(4,1)S(1)}, s32[]{:S(2)}) async-start(s8[5242880]{0:T(1024)(128)(4,1)} %bitcast.192), calls=%async_computation.22 | async-start | bytes 8388608
  591.7 11.0 %slice-start.4 = ((s8[5242880]{0:T(1024)(128)(4,1)}), s8[1048576]{0:T(1024)(128)(4,1)S(1)}, s32[]{:S(2)}) async-start(s8[5242880]{0:T(1024)(128)(4,1)} %bitcast.192), calls=%async_computation.23 | async-start | bytes 2097152
  602.7 5.7 copy-start.20
  610.6 10.2 copy-start.31
  635.0 147.5 %reduce-scatter.12.cloned.1.call-start = ((), (), s32[]{:S(2)}) async-start(), calls=%async_computation.15 | async-start | bytes 1769472 | tf_op jit(solution)/shard_map/reduce_scatter | solution.py:296
  635.0 9.3 copy-start.60
  635.1 9.3 copy-start.63
  644.3 11.3 %copy-start.51 = (f32[1024]{0:T(1024)S(1)}, f32[1024]{0:T(1024)}, u32[]{:S(2)}) copy-start(f32[1024]{0:T(1024)} %dynamic_slice.38) | copy-start | bytes 12292
  644.3 190.6 %reduce-scatter.18.cloned.1.call-start = ((), (), s32[]{:S(2)}) async-start(), calls=%async_computation.18 | async-start | bytes 2359296
  713.8 192.0 %reduce-scatter.14.cloned.1.call-start = ((), (), s32[]{:S(2)}) async-start(), calls=%async_computation.16 | async-start | bytes 2359296 | tf_op jit(solution)/shard_map/reduce_scatter | solution.py:299
  724.0 240.6 %all-gather.18.cloned.1.call-start = ((), (), s32[]{:S(2)}) async-start(), calls=%async_computation.12 | async-start | bytes 10485760 | tf_op jit(solution)/shard_map/all_gather | solution.py:247
  724.8 7.3 copy-start.57
  724.8 293.7 %reduce-scatter.10.cloned.1.call-start = ((), (), s32[]{:S(2)}) async-start(), calls=%async_computation.14 | async-start | bytes 6553600 | tf_op jit(solution)/shard_map/reduce_scatter | solution.py:287
  770.1 5.3 copy-start.50
  770.1 137.5 %all-to-all-start.1 = ((bf16[4,640,1024]{2,1,0:T(8,128)(2,1)}), bf16[4,640,1024]{2,1,0:T(8,128)(2,1)}, u32[]{:S(2)}, u32[]{:S(2)}) async-start(bf16[4,640,1024]{2,1,0:T(8,128)(2,1)} %bitcast.173), calls=%async_computation.1 | async-start | bytes 10485760 | tf_op jit(solution)/shard_map/all_to_all | solution.py:243
  964.7 53.8 %copy-start.1 = (f32[640,1024]{1,0:T(8,128)S(1)}, f32[640,1024]{1,0:T(8,128)}, u32[]{:S(2)}) copy-start(f32[640,1024]{1,0:T(8,128)} %param.48) | copy-start | bytes 7864324
  964.7 53.8 %copy-start.46 = (f32[640]{0:T(1024)S(1)}, f32[640]{0:T(1024)}, u32[]{:S(2)}) copy-start(f32[640]{0:T(1024)} %copy-done.45) | copy-start | bytes 7684
  964.7 53.8 %copy-start.49 = (f32[640]{0:T(1024)S(1)}, f32[640]{0:T(1024)}, u32[]{:S(2)}) copy-start(f32[640]{0:T(1024)} %copy-done.48) | copy-start | bytes 7684
  964.7 56.3 %copy-start.55 = (f32[1024]{0:T(1024)S(1)}, f32[1024]{0:T(1024)}, u32[]{:S(2)}) copy-start(f32[1024]{0:T(1024)} %param.62) | copy-start | bytes 12292
  964.7 56.3 %copy-start.56 = (f32[1024]{0:T(1024)S(1)}, f32[1024]{0:T(1024)}, u32[]{:S(2)}) copy-start(f32[1024]{0:T(1024)} %param.58) | copy-start | bytes 12292
  (19 other events, 49.4 us)
Sparse Core Ops, SparseCore 0:
  10.8 50.6 all-gather.9
  63.7 39.1 all-gather.7
  104.5 40.4 all-gather.19
  146.9 49.4 all-gather.13
  198.3 49.5 all-gather.15
  249.3 20.7 all-gather.11
  635.1 61.7 reduce-scatter.15
  700.7 63.8 reduce-scatter.11
  768.2 66.6 reduce-scatter.17
  838.9 66.9 reduce-scatter.13
  907.4 57.2 all-gather.17
  967.1 51.3 reduce-scatter.9
where the time goes:
time: 1080 us
  matrix products  555 us (51%)
  waiting for transfers between devices  283 us (26%)
  blocking collectives  93.6 us (9%)
  other arithmetic  88.5 us (8%)
  local copies, waits for them, and re-layouts  37.3 us (3%)
  between operations  15.5 us (1%)
    dot_general x5, matrix products, backward_tree(): jnp.einsum('hqk,qhd->khd', score_grad, queries[row_start:row_end], prefer...  155 us
    dot_general x5, matrix products, backward_tree(): jnp.einsum('hqk,khd->qhd', score_grad, key_rows[:key_end], preferred_elem...  142 us
    reduce_scatter x1, waiting for transfers between devices, local(): lax.psum_scatter(fc_weight_part.astype(jnp.bfloat16), 'dp', scatter_dimen...  69 us
    dot_general x4, matrix products, contract_last(): lax.dot_general(left, right, (((1,), (1,)), ((), ())), preferred_element_...  60.6 us
    all_gather x1, waiting for transfers between devices, local(): lax.all_gather(out_whole, 'tensor', axis=0, tiled=True)  57.1 us
    unnamed x14, waiting for transfers between devices  52.2 us
    reduce_scatter x1, waiting for transfers between devices, local(): lax.psum_scatter(grad_sent_part.astype(jnp.bfloat16), 'tensor', scatter_d...  41.9 us
    psum x1, blocking collectives, local(): lax.psum((gain_attn_part, shift_attn_part, gain_mlp_part, shift_mlp_part,...  40.9 us
  transfers between devices with their start and end apart: 13, of which 6 were waited for; matrix products, arithmetic and copies ran while one was open for 61% of the time, Pallas kernels for 0%

commit v1 on v0

--- a/solution.py
+++ b/solution.py
@@ -1,3 +1,4 @@
+import functools
 import jax
 import jax.numpy as jnp
 from jax import lax
@@ -10,6 +11,27 @@
 TREE = 2560
 eps_norm = 1e-05
 masked_score = -1e30
+
+
+def press_row(local_values, mesh_dim, array_axis):
+    value_now = lax.axis_size(mesh_dim)
+    m_next = lax.axis_index(mesh_dim)
+    view_out, part_next, z_new = (value_now, m_next, local_values.shape[array_axis])
+    val2, z1 = (local_values, 1)
+    while z1 < view_out:
+        val2 = jnp.concatenate(
+            [
+                val2,
+                lax.ppermute(val2, mesh_dim, [(t, (t - z1) % view_out) for t in range(view_out)]),
+            ],
+            axis=array_axis,
+        )
+        z1 = 2 * z1
+    arr_next = jnp.roll(val2, part_next * z_new, axis=array_axis)
+    return arr_next
+
+
+touch_the_sources_all = functools.partial(press_row, mesh_dim="dp", array_axis=1)
 
 
 def contract_first(left, right):
@@ -211,7 +233,7 @@
     qkv_whole, fc_whole, dense_whole, out_whole = (
         lax.all_gather(qkv_weight.astype(jnp.bfloat16), "dp", axis=0, tiled=True),
         lax.all_gather(fc_weight.astype(jnp.bfloat16), "dp", axis=0, tiled=True),
-        lax.all_gather(dense_weight.astype(jnp.bfloat16), "dp", axis=1, tiled=True),
+        touch_the_sources_all(dense_weight.astype(jnp.bfloat16)),
         lax.all_gather(out_weight.astype(jnp.bfloat16), "dp", axis=1, tiled=True),
     )
     sent_float = sent_group.astype(jnp.float32)

time: 1080 us -> 1090 us (level)
  blocking collectives: 93.6 us -> 60.6 us
  waiting for transfers between devices: 283 us -> 313 us
    all_gather x1 -> x0, blocking collectives: 33 us -> none  [local(): lax.all_gather(dense_weight.astype(jnp.bfloat16), 'dp', axis=1, tiled=True)]
    ppermute x0 -> x3, waiting for transfers between devices: none -> 25.2 us  [press_row(): lax.ppermute(val2, mesh_dim, [(t, (t - z1) % view_out) for t in range(vie...]
  transfers between devices with their start and end apart: 13 -> 16, of which waited for: 6 -> 8; matrix products, arithmetic and copies ran while one was open for 61% -> 61% of each run, Pallas kernels for 0% -> 0%
where the time goes in v1:
time: 1090 us; the launch traced here: 1080 us
  matrix products  556 us (51%)
  waiting for transfers between devices  313 us (29%)
  other arithmetic  88.2 us (8%)
  blocking collectives  60.6 us (6%)
  local copies, waits for them, and re-layouts  38.2 us (4%)
  between operations  15.5 us (1%)
  starting transfers between devices  12.8 us (1%)
    dot_general x5, matrix products, backward_tree(): jnp.einsum('hqk,qhd->khd', score_grad, queries[row_start:row_end], prefer...  155 us
    dot_general x5, matrix products, backward_tree(): jnp.einsum('hqk,khd->qhd', score_grad, key_rows[:key_end], preferred_elem...  142 us
    reduce_scatter x1, waiting for transfers between devices, local(): lax.psum_scatter(fc_weight_part.astype(jnp.bfloat16), 'dp', scatter_dimen...  68.8 us
    dot_general x4, matrix products, contract_last(): lax.dot_general(left, right, (((1,), (1,)), ((), ())), preferred_element_...  60.7 us
    all_gather x1, waiting for transfers between devices, local(): lax.all_gather(out_whole, 'tensor', axis=0, tiled=True)  57.2 us
    unnamed x14, waiting for transfers between devices  52 us
    reduce_scatter x1, waiting for transfers between devices, local(): lax.psum_scatter(grad_sent_part.astype(jnp.bfloat16), 'tensor', scatter_d...  41.9 us
    psum x1, blocking collectives, local(): lax.psum((gain_attn_part, shift_attn_part, gain_mlp_part, shift_mlp_part,...  40.9 us
  transfers between devices with their start and end apart: 16, of which 8 were waited for; matrix products, arithmetic and copies ran while one was open for 61% of the time, Pallas kernels for 0%

profile of v1, /device:TPU:0, one launch (start us, length us, event | category | flops | bytes accessed | tf_op | source)
XLA Modules:
  0.0 1084.9 jit_solution(4160105223393051153)
XLA Ops:
  16.4 6.1 collective-permute-start
  28.7 9.0 fusion.112
  39.4 4.1 collective-permute-done.1
  46.2 21.1 %collective-permute-done.2 = bf16[256,512]{1,0:T(8,128)(2,1)S(1)} collective-permute-done((bf16[256,512]{1,0:T(8,128)(2,1)S(1)}, bf16[256,512]{1,0:T(8,128)(2,1)S(1)}, u32[]{:S(2)}, u32[]{:S(2)}) %collective-permute-start.2) | collective-permute-done | bytes 262176 | tf_op jit(solution)/shard_map/ppermute | solution.py:25
  68.7 39.9 %all-gather.8.cloned.1.call-done = bf16[2560,1024]{1,0:T(8,128)(2,1)} async-done(((bf16[640,1024]{1,0:T(8,128)(2,1)}), bf16[2560,1024]{1,0:T(8,128)(2,1)}) %all-gather.8.cloned.1.call-update) | async-done | bytes 5242896 | tf_op jit(solution)/shard_map/all_gather | solution.py:232
  108.6 6.9 convolution_add_fusion
  115.5 2.5 copy.67
  122.2 28.5 %all-gather.20.cloned.1.call-done = bf16[2560,1024]{1,0:T(8,128)(2,1)} async-done(((bf16[640,1024]{1,0:T(8,128)(2,1)}), bf16[2560,1024]{1,0:T(8,128)(2,1)}) %all-gather.20.cloned.1.call-update) | async-done | bytes 5242896 | tf_op jit(solution)/shard_map/all_gather | solution.py:277
  150.6 4.3 fusion.166
  160.8 3.9 fusion.254
  166.8 8.7 fusion.208
  175.4 9.8 fusion.205
  185.2 4.3 fusion.214
  191.3 5.6 fusion.249
  198.6 3.2 copy-done.2
  201.9 2.4 exponential_reduce_fusion.3
  204.3 18.1 %fusion.219 = f32[2560,4,64]{0,2,1:T(8,128)} fusion(f32[2560,4,64]{0,2,1:T(8,128)} %fusion.205, f32[4,512,1024]{2,1,0:T(8,128)} %fusion.249, f32[4,512,1024]{2,1,0:T(8,128)} %copy-done.2, f32[4,512]{1,0:T(4,128)S(1)} %log_add_fusion.3, pred[512,1024]{1,0:T(8,128)(4,1)S(1)} %and_or_fusion, bf16[2560,4,48]{0,2,1:T(8,128)(2,1)S(1)} %slice.741, ...), kind=kOutput, calls=%fused_computation.212 | convolution fusion | flops 292555776 | bytes 36454400 | tf_op jit(solution)/shard_map/while/body/eval_jaxpr/hqk,khd->qhd/dot_general | solution.py:186
  222.4 23.3 %fusion.198 = f32[2560,4,64]{0,2,1:T(8,128)} fusion(f32[2560,4,64]{0,2,1:T(8,128)} %scatter-add.14, f32[4,512,1024]{2,1,0:T(8,128)} %fusion.249, f32[4,512,1024]{2,1,0:T(8,128)} %copy-done.2, f32[4,512]{1,0:T(4,128)S(1)} %log_add_fusion.3, pred[512,1024]{1,0:T(8,128)(4,1)S(1)} %and_or_fusion, bf16[2560,4,48]{0,2,1:T(8,128)(2,1)S(1)} %slice.742, ...), kind=kOutput, calls=%fused_computation.188 | convolution fusion | flops 292293632 | bytes 38027264 | tf_op jit(solution)/shard_map/while/body/eval_jaxpr/hqk,qhd->khd/dot_general | solution.py:191
  245.7 10.1 fusion.248
  255.8 9.0 fusion.247
  264.8 8.6 fusion.246
  273.4 5.5 fusion.10
  279.0 7.3 exponential_reduce_fusion
  286.4 5.5 fusion.8
  292.0 7.1 exponential_reduce_fusion.2
  299.4 5.5 fusion.9
  304.9 7.1 exponential_reduce_fusion.1
  312.4 40.8 %fusion.140 = f32[2560,4,64]{0,2,1:T(8,128)} fusion(f32[4,512,2560]{2,1,0:T(8,128)} %fusion.247, f32[4,512,2560]{2,1,0:T(8,128)} %copy-done.4, f32[4,512]{1,0:T(4,128)S(1)} %log_add_fusion.1, pred[512,2560]{1,0:T(8,128)(4,1)} %get-tuple-element.356, bf16[2560,4,48]{0,2,1:T(8,128)(2,1)S(1)} %slice.742, bf16[2560,4,16]{0,2,1:T(8,128)(2,1)S(1)} %get-tuple-element.343), kind=kOutput, calls=%fused_computation.132 | convolution fusion | flops 729289216 | bytes 90456064 | tf_op jit(solution)/shard_map/while/body/eval_jaxpr/hqk,qhd->khd/dot_general | solution.py:191
  353.2 38.3 %fusion.237 = f32[2560,4,64]{0,2,1:T(8,128)} fusion(f32[2560,4,64]{0,2,1:T(8,128)} %fusion.219, f32[4,512,2560]{2,1,0:T(8,128)} %fusion.248, f32[4,512,2560]{2,1,0:T(8,128)} %copy-done.5, f32[4,512]{1,0:T(4,128)S(1)} %log_add_fusion.2, pred[512,2560]{1,0:T(8,128)(4,1)} %get-tuple-element.355, bf16[2560,4,48]{0,2,1:T(8,128)(2,1)S(1)} %slice.741, ...), kind=kOutput, calls=%fused_computation.218 | convolution fusion | flops 731386368 | bytes 88358912 | tf_op jit(solution)/shard_map/while/body/eval_jaxpr/hqk,khd->qhd/dot_general | solution.py:186
  391.5 38.0 %fusion.231 = f32[2560,4,64]{0,2,1:T(8,128)} fusion(f32[2560,4,64]{0,2,1:T(8,128)} %fusion.237, f32[4,512,2560]{2,1,0:T(8,128)} %fusion.247, f32[4,512,2560]{2,1,0:T(8,128)} %copy-done.4, f32[4,512]{1,0:T(4,128)S(1)} %log_add_fusion.1, pred[512,2560]{1,0:T(8,128)(4,1)} %get-tuple-element.356, bf16[2560,4,48]{0,2,1:T(8,128)(2,1)S(1)} %slice.741, ...), kind=kOutput, calls=%fused_computation.216 | convolution fusion | flops 731386368 | bytes 88358912 | tf_op jit(solution)/shard_map/while/body/eval_jaxpr/hqk,khd->qhd/dot_general | solution.py:186
  429.5 40.7 %fusion.137 = f32[2560,4,64]{0,2,1:T(8,128)} fusion(bf16[512,4,64]{0,2,1:T(8,128)(2,1)S(1)} %copy-done.43, f32[4,512,2560]{2,1,0:T(8,128)} %fusion.246, f32[4,512,2560]{2,1,0:T(8,128)} %copy-done.3, f32[4,512]{1,0:T(4,128)S(1)} %log_add_fusion, pred[512,2560]{1,0:T(8,128)(4,1)} %get-tuple-element.354), kind=kOutput, calls=%fused_computation.131 | convolution fusion | flops 728764928 | bytes 46145536 | tf_op jit(solution)/shard_map/while/body/eval_jaxpr/hqk,qhd->khd/dot_general | solution.py:191
  470.2 37.9 %fusion.225 = f32[2560,4,64]{0,2,1:T(8,128)} fusion(f32[2560,4,64]{0,2,1:T(8,128)} %fusion.231, f32[4,512,2560]{2,1,0:T(8,128)} %fusion.246, f32[4,512,2560]{2,1,0:T(8,128)} %copy-done.3, f32[4,512]{1,0:T(4,128)S(1)} %log_add_fusion, pred[512,2560]{1,0:T(8,128)(4,1)} %get-tuple-element.354, bf16[2560,4,48]{0,2,1:T(8,128)(2,1)S(1)} %slice.741, ...), kind=kOutput, calls=%fused_computation.214 | convolution fusion | flops 731386368 | bytes 88358912 | tf_op jit(solution)/shard_map/while/body/eval_jaxpr/hqk,khd->qhd/dot_general | solution.py:186
  508.1 41.6 %fusion.156 = f32[2560,4,64]{0,2,1:T(8,128)} fusion(f32[2560,4,64]{0,2,1:T(8,128)} %fusion.137, f32[2560,4,64]{0,2,1:T(8,128)} %fusion.140, f32[2560,4,64]{0,2,1:T(8,128)} %fusion.198, f32[4,512,2560]{2,1,0:T(8,128)} %fusion.248, f32[4,512,2560]{2,1,0:T(8,128)} %copy-done.5, f32[4,512]{1,0:T(4,128)S(1)} %log_add_fusion.2, ...), kind=kOutput, calls=%fused_computation.143 | convolution fusion | flops 731255296 | bytes 98320384 | tf_op jit(solution)/shard_map/while/body/eval_jaxpr/hqk,qhd->khd/dot_general | solution.py:191
  549.8 2.7 slice.646
  552.5 2.6 slice.642
  555.1 2.4 slice_multiply_fusion.3
  557.8 5.0 fusion.194
  566.3 11.7 %fusion.149 = f32[2560,4,64]{0,2,1:T(8,128)} fusion(f32[2560,4,64]{0,2,1:T(8,128)S(1)} %fusion.194, bf16[512,4,64]{0,2,1:T(8,128)(2,1)S(1)} %bitcast.186, f32[4,512,2560]{2,1,0:T(8,128)} %copy-done.5, f32[4,512]{1,0:T(4,128)S(1)} %log_add_fusion.2, pred[512,2560]{1,0:T(8,128)(4,1)S(1)} %copy-done.13), kind=kOutput, calls=%fused_computation.140 | convolution fusion | flops 692715520 | bytes 27795456 | tf_op jit(solution)/shard_map/while/body/eval_jaxpr/hqk,qhd->khd/dot_general | solution.py:178
  578.0 9.8 fusion.213
  587.9 10.4 fusion.212
  598.3 9.8 fusion.211
  617.2 10.2 fusion.148
  627.4 10.4 fusion.147
  641.7 9.2 fusion.187
  651.0 11.2 %fusion.161 = f32[2560,1024]{1,0:T(8,128)} fusion(bf16[1024,1024]{1,0:T(8,128)(2,1)} %all-gather.14.cloned.1.call-done, bf16[2560,1024]{1,0:T(8,128)(2,1)} %all-gather.8.cloned.1.call-done, f32[1024]{0:T(1024)S(1)} %copy-done.60, f32[1024]{0:T(1024)S(1)} %copy-done.63), kind=kOutput, calls=%fused_computation.145 | convolution fusion | flops 5379194880 | bytes 17833984 | tf_op jit(solution)/shard_map/dot_general | solution.py:261
  662.2 33.9 %convert_reduce_fusion = (f32[1024]{0:T(1024)S(1)}, bf16[2560,1024]{1,0:T(8,128)(2,1)}, f32[2560,1024]{1,0:T(8,128)}) fusion(f32[2560,1024]{1,0:T(8,128)} %fusion.161, f32[1024]{0:T(1024)S(1)} %copy-done.51, bf16[2560,1024]{1,0:T(8,128)(2,1)} %all-gather.20.cloned.1.call-done, bf16[1024,1024]{1,0:T(8,128)(2,1)} %all-gather.16.cloned.1.call-done), kind=kOutput, calls=%fused_computation.47 | convolution fusion | flops 5565316096 | bytes 33562624 | tf_op jit(solution)/shard_map/dot_general | solution.py:44
  696.1 12.3 %multiply_convert_fusion.3 = bf16[2560,1024]{1,0:T(8,128)(2,1)} fusion(f32[2560,1024]{1,0:T(8,128)} %get-tuple-element.316, f32[2560,1024]{1,0:T(8,128)} %fusion.161, f32[1024]{0:T(1024)S(1)} %copy-done.51), kind=kLoop, calls=%fused_computation.51 | loop fusion | flops 10485760 | bytes 26218496 | tf_op jit(solution)/shard_map/convert_element_type | solution.py:262
  708.4 9.4 convolution_convert_fusion.1
  717.8 2.6 copy.64
  720.5 10.2 fusion.184
  731.4 7.2 fusion.337
  738.7 15.2 %fusion.329 = (f32[1024]{0:T(1024)S(1)}, f32[1024]{0:T(1024)S(1)}, bf16[2560,1024]{1,0:T(8,128)(2,1)}, f32[1024]{0:T(1024)S(1)}, f32[1024]{0:T(1024)S(1)}) fusion(bf16[2560,1024]{1,0:T(8,128)(2,1)} %all-gather.8.cloned.1.call-done, f32[1024]{0:T(1024)S(1)} %copy-done.63, f32[2560,1024]{1,0:T(8,128)S(1)} %fusion.337, f32[1024]{0:T(1024)S(1)} %copy-done.62, ...), kind=kOutput, calls=%fused_computation.344 | convolution fusion | flops 5397540864 | bytes 28336128 | tf_op jit(solution)/shard_map/dot_general | solution.py:44
  757.0 19.7 %all_to_all.29 = bf16[4,640,256]{2,1,0:T(8,128)(2,1)S(1)} all-to-all(bf16[4,640,256]{2,1,0:T(8,128)(2,1)S(1)} %copy.52), channel_id=1, replica_groups=mesh['dp'=8,'tensor'=4] {'tensor'}, dimensions={0} | all-to-all | bytes 2621440 | tf_op jit(solution)/shard_map/all_to_all | solution.py:264
  776.7 5.3 all-to-all-start.1
  782.7 4.8 convert_reduce_fusion.2
  790.8 50.5 %reduce-scatter.18.cloned.1.call-done = bf16[128,1024]{1,0:T(8,128)(2,1)} async-done(((bf16[1024,1024]{1,0:T(8,128)(2,1)}), bf16[128,1024]{1,0:T(8,128)(2,1)}) %reduce-scatter.18.cloned.1.call-update) | async-done | bytes 262160
  843.3 68.8 %reduce-scatter.14.cloned.1.call-done = bf16[128,1024]{1,0:T(8,128)(2,1)} async-done(((bf16[1024,1024]{1,0:T(8,128)(2,1)}), bf16[128,1024]{1,0:T(8,128)(2,1)}) %reduce-scatter.14.cloned.1.call-update) | async-done | bytes 262160 | tf_op jit(solution)/shard_map/reduce_scatter | solution.py:321
  913.8 57.2 %all-gather.18.cloned.1.call-done = bf16[4096,1024]{1,0:T(8,128)(2,1)} async-done(((bf16[1024,1024]{1,0:T(8,128)(2,1)}), bf16[4096,1024]{1,0:T(8,128)(2,1)}) %all-gather.18.cloned.1.call-update) | async-done | bytes 8388624 | tf_op jit(solution)/shard_map/all_gather | solution.py:269
  971.0 11.9 %convert_reduce_fusion.1 = f32[640,1024]{1,0:T(8,128)} fusion(bf16[4,1024,1024]{2,1,0:T(8,128)(2,1)} %bitcast.193, bf16[4,640,1024]{2,1,0:T(8,128)(2,1)} %all-to-all-done.1), kind=kOutput, calls=%fused_computation.50 | convolution fusion | flops 5375918080 | bytes 16252928 | tf_op jit(solution)/shard_map/rgc,gcd->grd/dot_general | solution.py:52
  982.9 41.9 %reduce-scatter.10.cloned.1.call-done = bf16[640,1024]{1,0:T(8,128)(2,1)} async-done(((bf16[2560,1024]{1,0:T(8,128)(2,1)}), bf16[640,1024]{1,0:T(8,128)(2,1)}) %reduce-scatter.10.cloned.1.call-update) | async-done | bytes 1310736 | tf_op jit(solution)/shard_map/reduce_scatter | solution.py:309
  1024.8 2.4 convert_reduce_fusion.4
  1027.3 6.7 multiply_reduce_fusion.7
  1033.9 40.9 %all-reduce.2 = (f32[1024]{0:T(1024)}, f32[1024]{0:T(1024)}, f32[1024]{0:T(1024)}, f32[1024]{0:T(1024)}, f32[3072]{0:T(1024)}, /*index=5*/f32[1024]{0:T(1024)S(1...) all-reduce(f32[1024]{0:T(1024)S(1)} %get-tuple-element.322, ...), channel_id=1, replica_groups=mesh['dp'=8,'tensor'=4] {'dp','tensor'}, use_global_device_ids=true, to_apply=%region_23.24 | all-reduce | flops 12291 | bytes 98328 | tf_op jit(solution)/shard_map/psum | solution.py:349
  1074.8 2.4 fusion.273
  (259 shorter events, 65.9 us)
Async XLA Ops:
  7.2 6.2 copy-start
  7.2 61.5 %all-gather.10.cloned.1.call-start = ((), (), s32[]{:S(2)}) async-start(), calls=%async_computation.8 | async-start | bytes 1769472 | tf_op jit(solution)/shard_map/all_gather | solution.py:234
  9.1 99.5 %all-gather.8.cloned.1.call-start = ((), (), s32[]{:S(2)}) async-start(), calls=%async_computation.7 | async-start | bytes 6553600 | tf_op jit(solution)/shard_map/all_gather | solution.py:232
  11.1 13.3 %copy-start.42 = (s32[2560]{0:T(1024)S(1)}, s32[2560]{0:T(1024)}, u32[]{:S(2)}) copy-start(s32[2560]{0:T(1024)} %param.49) | copy-start | bytes 30724
  11.2 15.1 %copy-start.47 = (s32[2560]{0:T(1024)S(1)}, s32[2560]{0:T(1024)}, u32[]{:S(2)}) copy-start(s32[2560]{0:T(1024)} %param.50) | copy-start | bytes 30724
  13.4 24.4 %copy-start.48 = (f32[640]{0:T(1024)}, f32[640]{0:T(1024)S(1)}, u32[]{:S(2)}) copy-start(f32[640]{0:T(1024)S(1)} %add_rsqrt_fusion) | copy-start | bytes 7684
  14.8 23.5 %slice-start.2 = ((s32[2560]{0:T(1024)}), s32[1024]{0:T(1024)S(1)}, s32[]{:S(2)}) async-start(s32[2560]{0:T(1024)} %param.49), calls=%async_computation.21 | async-start | bytes 8192 | tf_op jit(solution)/shard_map/while/body/eval_jaxpr/slice | solution.py:125
  14.8 135.8 %all-gather.20.cloned.1.call-start = ((), (), s32[]{:S(2)}) async-start(), calls=%async_computation.13 | async-start | bytes 6553600 | tf_op jit(solution)/shard_map/all_gather | solution.py:277
  15.5 635.4 %all-gather.14.cloned.1.call-start = ((), (), s32[]{:S(2)}) async-start(), calls=%async_computation.10 | async-start | bytes 2359296 | tf_op jit(solution)/shard_map/all_gather | solution.py:235
  16.3 645.9 %all-gather.16.cloned.1.call-start = ((), (), s32[]{:S(2)}) async-start(), calls=%async_computation.11 | async-start | bytes 2359296 | tf_op jit(solution)/shard_map/all_gather | solution.py:237
  16.4 21.3 %collective-permute-start = (bf16[256,128]{1,0:T(8,128)(2,1)S(1)}, bf16[256,128]{1,0:T(8,128)(2,1)S(1)}, u32[]{:S(2)}, u32[]{:S(2)}) collective-permute-start(bf16[256,128]{1,0:T(8,128)(2,1)S(1)} %get-tuple-element.320), channel_id=1, source_target_pairs={{0,28},{4,0},{8,4},{12,8},{16,12},{20,16},{24,20},{28,24},{1,29},{... | collective-permute-start | bytes 196616 | tf_op jit(solution)/shard_map/ppermute | solution.py:25
  24.3 84.3 %copy-start.58 = (f32[1024]{0:T(1024)S(1)}, f32[1024]{0:T(1024)}, u32[]{:S(2)}) copy-start(f32[1024]{0:T(1024)} %param.52) | copy-start | bytes 12292
  24.3 84.3 %copy-start.61 = (f32[1024]{0:T(1024)S(1)}, f32[1024]{0:T(1024)}, u32[]{:S(2)}) copy-start(f32[1024]{0:T(1024)} %param.51) | copy-start | bytes 12292
  24.3 758.4 %all-gather.12.cloned.1.call-start = ((), (), s32[]{:S(2)}) async-start(), calls=%async_computation.9 | async-start | bytes 2621440 | tf_op jit(solution)/shard_map/all_gather | solution.py:268
  37.8 5.7 collective-permute-start.1
  39.4 183.0 %copy-start.14 = (pred[512,1024]{1,0:T(8,128)(4,1)}, pred[512,1024]{1,0:T(8,128)(4,1)S(1)}, u32[]{:S(2)}) copy-start(pred[512,1024]{1,0:T(8,128)(4,1)S(1)} %and_or_fusion) | copy-start | bytes 1572868
  43.5 23.8 %collective-permute-start.2 = (bf16[256,512]{1,0:T(8,128)(2,1)S(1)}, bf16[256,512]{1,0:T(8,128)(2,1)S(1)}, u32[]{:S(2)}, u32[]{:S(2)}) collective-permute-start(bf16[256,512]{1,0:T(8,128)(2,1)S(1)} %pad_maximum_fusion.4), channel_id=1, source_target_pairs={{0,16},{4,20},{8,24},{12,28},{16,0},{20,4},{24,8},{28,12},{1,17},{... | collective-permute-start | bytes 786440 | tf_op jit(solution)/shard_map/ppermute | solution.py:25
  68.3 719.2 %reduce-scatter.16.cloned.1.call-start = ((), (), s32[]{:S(2)}) async-start(), calls=%async_computation.17 | async-start | bytes 589824
  150.6 5.3 copy-start.19
  150.6 5.3 copy-start.21
  150.6 5.3 copy-start.23
  150.6 5.3 copy-start.24
  150.6 5.4 copy-start.25
  150.6 5.4 copy-start.26
  185.2 6.1 copy-start.36
  204.3 18.1 %copy-start.52 = (f32[4,512]{1,0:T(4,128)}, f32[4,512]{1,0:T(4,128)S(1)}, u32[]{:S(2)}) copy-start(f32[4,512]{1,0:T(4,128)S(1)} %log_add_fusion.3) | copy-start | bytes 24580
  222.4 23.3 %copy-start.34 = (bf16[512,256]{0,1:T(8,128)(2,1)S(1)}, bf16[512,256]{0,1:T(8,128)(2,1)}, u32[]{:S(2)}) copy-start(bf16[512,256]{0,1:T(8,128)(2,1)} %get-tuple-element.336) | copy-start | bytes 786436
  245.7 10.1 copy-start.6
  245.7 10.1 copy-start.32
  255.8 9.0 copy-start.30
  264.8 8.6 copy-start.43
  279.0 7.4 copy-start.3
  291.9 7.4 copy-start.5
  304.9 7.4 copy-start.4
  508.1 47.0 %copy-start.22 = (f32[2560,16]{0,1:T(8,128)S(1)}, f32[2560,16]{0,1:T(8,128)}, u32[]{:S(2)}) copy-start(f32[2560,16]{0,1:T(8,128)} %get-tuple-element.393) | copy-start | bytes 491524
  549.7 7.7 copy-start.40
  549.8 8.0 copy-start.15
  549.8 8.0 copy-start.37
  549.8 8.0 copy-start.53
  555.1 7.8 slice-start
  557.8 5.8 copy-start.7
  557.8 6.1 copy-start.27
  578.0 9.8 copy-start.12
  587.9 10.4 copy-start.11
  587.9 21.4 %slice-start.3 = ((s8[5242880]{0:T(1024)(128)(4,1)}), s8[4194304]{0:T(1024)(128)(4,1)S(1)}, s32[]{:S(2)}) async-start(s8[5242880]{0:T(1024)(128)(4,1)} %bitcast.194), calls=%async_computation.22 | async-start | bytes 8388608
  598.3 11.0 %slice-start.4 = ((s8[5242880]{0:T(1024)(128)(4,1)}), s8[1048576]{0:T(1024)(128)(4,1)S(1)}, s32[]{:S(2)}) async-start(s8[5242880]{0:T(1024)(128)(4,1)} %bitcast.194), calls=%async_computation.23 | async-start | bytes 2097152
  609.2 5.7 copy-start.20
  617.2 10.2 copy-start.31
  641.6 147.6 %reduce-scatter.12.cloned.1.call-start = ((), (), s32[]{:S(2)}) async-start(), calls=%async_computation.15 | async-start | bytes 1769472 | tf_op jit(solution)/shard_map/reduce_scatter | solution.py:318
  641.6 9.3 copy-start.60
  641.6 9.3 copy-start.63
  650.9 11.3 %copy-start.51 = (f32[1024]{0:T(1024)S(1)}, f32[1024]{0:T(1024)}, u32[]{:S(2)}) copy-start(f32[1024]{0:T(1024)} %dynamic_slice.43) | copy-start | bytes 12292
  650.9 190.4 %reduce-scatter.18.cloned.1.call-start = ((), (), s32[]{:S(2)}) async-start(), calls=%async_computation.18 | async-start | bytes 2359296
  720.4 191.6 %reduce-scatter.14.cloned.1.call-start = ((), (), s32[]{:S(2)}) async-start(), calls=%async_computation.16 | async-start | bytes 2359296 | tf_op jit(solution)/shard_map/reduce_scatter | solution.py:321
  730.6 240.3 %all-gather.18.cloned.1.call-start = ((), (), s32[]{:S(2)}) async-start(), calls=%async_computation.12 | async-start | bytes 10485760 | tf_op jit(solution)/shard_map/all_gather | solution.py:269
  731.4 7.3 copy-start.57
  731.4 293.4 %reduce-scatter.10.cloned.1.call-start = ((), (), s32[]{:S(2)}) async-start(), calls=%async_computation.14 | async-start | bytes 6553600 | tf_op jit(solution)/shard_map/reduce_scatter | solution.py:309
  776.7 5.4 copy-start.50
  776.7 137.1 %all-to-all-start.1 = ((bf16[4,640,1024]{2,1,0:T(8,128)(2,1)}), bf16[4,640,1024]{2,1,0:T(8,128)(2,1)}, u32[]{:S(2)}, u32[]{:S(2)}) async-start(bf16[4,640,1024]{2,1,0:T(8,128)(2,1)} %bitcast.175), calls=%async_computation.1 | async-start | bytes 10485760 | tf_op jit(solution)/shard_map/all_to_all | solution.py:265
  971.0 53.8 %copy-start.1 = (f32[640,1024]{1,0:T(8,128)S(1)}, f32[640,1024]{1,0:T(8,128)}, u32[]{:S(2)}) copy-start(f32[640,1024]{1,0:T(8,128)} %param.48) | copy-start | bytes 7864324
  971.0 53.8 %copy-start.46 = (f32[640]{0:T(1024)S(1)}, f32[640]{0:T(1024)}, u32[]{:S(2)}) copy-start(f32[640]{0:T(1024)} %copy-done.45) | copy-start | bytes 7684
  971.0 53.8 %copy-start.49 = (f32[640]{0:T(1024)S(1)}, f32[640]{0:T(1024)}, u32[]{:S(2)}) copy-start(f32[640]{0:T(1024)} %copy-done.48) | copy-start | bytes 7684
  971.0 56.3 %copy-start.55 = (f32[1024]{0:T(1024)S(1)}, f32[1024]{0:T(1024)}, u32[]{:S(2)}) copy-start(f32[1024]{0:T(1024)} %param.62) | copy-start | bytes 12292
  971.0 56.3 %copy-start.56 = (f32[1024]{0:T(1024)S(1)}, f32[1024]{0:T(1024)}, u32[]{:S(2)}) copy-start(f32[1024]{0:T(1024)} %param.58) | copy-start | bytes 12292
  (22 other events, 65.1 us)
Sparse Core Ops, SparseCore 0:
  10.8 56.6 all-gather.9
  69.6 38.9 all-gather.7
  110.2 40.4 all-gather.19
  152.6 49.3 all-gather.13
  203.9 49.5 all-gather.15
  255.5 20.7 all-gather.11
  641.7 61.8 reduce-scatter.15
  707.4 63.7 reduce-scatter.11
  774.7 66.5 reduce-scatter.17
  845.2 66.7 reduce-scatter.13
  913.6 57.3 all-gather.17
  973.4 51.3 reduce-scatter.9
